TPU v7x, 512 devices: a whole 4x4x16 slice. The times are simulated.
512 devices in a mesh: region: 64 (over z, x), split: 8 (over y, core).
Axes of the slice: x: 4, y: 4, z: 16, core: 2. Of those that a mesh axis runs over, the one named last changes fastest.
Arguments:
- vectors: float32 [294912, 256], P(('region', 'split'))
- hessian: bfloat16 [1536, 12, 192, 192], P(('region', 'split')), may hold values from -0.125 to 0.125
- block_cols: int32 [1536, 12], P(('region', 'split')), may hold values from 0 to 35, as said below
- live_blocks: int32 [1536], P(('region', 'split')), may hold values from 6 to 12, as said below
- halo_lists: int32 [64, 2, 6], P('region'), may hold values from 0 to 23, as said below
- bounds: float32 [2], replicated, as said below
Outputs:
- basis: float32 [294912, 256], P(('region', 'split'))
- projected: float32 [256, 256], replicated
Inputs may be any that keep to these rules, and one draw needn't show every extreme that they name: `block_cols`: in each row the entries are distinct and entry 0 is the row's own block within its region; values below 24 name blocks of the row's region, 24 + j the j-th block received from the lower region, 30 + j the j-th from the upper region. `live_blocks`: the first block row of every region has all 12 blocks intact. `halo_lists`: each list holds distinct block indices within the region. bounds[0] < 0 < bounds[1].
All inputs are finite; a program needn't handle non-finite values.
Results may differ from a plain program's by a relative error of at most 0.0005.
The roundings to bfloat16 on the way count: a program that leaves them out, or rounds other values in their place, can miss the bound.
Values may be sent and summed in bfloat16 or wider, within the bound.
A program may use at most 64 MiB of HBM per device.

v0:
```python
import jax
import jax.numpy as jnp
from jax import lax
from jax.sharding import PartitionSpec as P


def shifted(value, axis, steps):
    count = lax.axis_size(axis)
    pairs = [(source, (source + steps) % count) for source in range(count)]
    return lax.ppermute(value, axis, pairs)


def apply_blocks(operand, hessian, block_cols, live_blocks, halo_lists):
    row_blocks = hessian.shape[0]
    block_size = hessian.shape[2]
    mode_count = operand.shape[1]
    shard_blocks = operand.reshape(row_blocks, block_size, mode_count)
    region = lax.all_gather(shard_blocks, "split", axis=0, tiled=True)
    send_lower = region[halo_lists[0, 0]]
    send_upper = region[halo_lists[0, 1]]
    from_lower = shifted(send_upper, "region", 1)
    from_upper = shifted(send_lower, "region", -1)
    candidates = jnp.concatenate([region, from_lower, from_upper], 0)
    picked = candidates[block_cols]
    used_mask = lax.broadcasted_iota(jnp.int32, block_cols.shape, 1) < live_blocks[:, None]
    picked = jnp.where(used_mask[:, :, None, None], picked, jnp.zeros((), jnp.bfloat16))
    product = jnp.einsum("rkij,rkjm->rim", hessian, picked, preferred_element_type=jnp.float32)
    return product.reshape(row_blocks * block_size, mode_count)


def local(vectors, hessian, block_cols, live_blocks, halo_lists, bounds):
    centre = 0.5 * (bounds[0] + bounds[1])
    half_width = 0.5 * (bounds[1] - bounds[0])
    first = apply_blocks(vectors.astype(jnp.bfloat16), hessian, block_cols, live_blocks, halo_lists)
    filtered_one = (first - centre * vectors) / half_width
    second = apply_blocks(
        filtered_one.astype(jnp.bfloat16), hessian, block_cols, live_blocks, halo_lists
    )
    filtered_two = 2.0 * (second - centre * filtered_one) / half_width - vectors
    image = apply_blocks(
        filtered_two.astype(jnp.bfloat16), hessian, block_cols, live_blocks, halo_lists
    )
    total_rows = vectors.shape[0] * lax.axis_size("region") * lax.axis_size("split")
    contract = (((0,), (0,)), ((), ()))
    gram_part = lax.dot_general(
        filtered_two, filtered_two, contract, precision=lax.Precision.HIGHEST
    )
    cross_part = lax.dot_general(filtered_two, image, contract, precision=lax.Precision.HIGHEST)
    gram, cross = lax.psum((gram_part, cross_part), ("region", "split"))
    gram = gram / total_rows
    cross = cross / total_rows
    lower = jnp.linalg.cholesky(gram)
    basis = jax.scipy.linalg.solve_triangular(lower, filtered_two.T, lower=True).T
    partial_left = jax.scipy.linalg.solve_triangular(lower, cross, lower=True)
    projected = jax.scipy.linalg.solve_triangular(lower, partial_left.T, lower=True).T
    return (basis, projected)


def solution(mesh):
    placed = (
        P(("region", "split"), None),
        P(("region", "split"), None, None, None),
        P(("region", "split"), None),
        P(("region", "split")),
        P("region", None, None),
        P(),
    )
    return jax.shard_map(
        local,
        mesh=mesh,
        in_specs=placed,
        out_specs=(P(("region", "split"), None), P()),
        check_vma=False,
    )
```

profile of v0, /device:TPU:1, one launch (start us, length us, event | category | flops | bytes accessed | tf_op | source)
XLA Modules:
  0.0 814.2 jit_solution(8782221556383976657)
XLA Ops:
  10.1 39.6 %all-gather.4.cloned.1.call-done = bf16[24,192,256]{2,1,0:T(8,128)(2,1)} async-done(((bf16[3,192,256]{2,1,0:T(8,128)(2,1)}), bf16[24,192,256]{2,1,0:T(8,128)(2,1)}) %all-gather.4.cloned.1.call-update) | async-done | bytes 2359312 | tf_op jit(solution)/shard_map/all_gather | solution.py:18
  49.7 3.1 gather_fusion
  52.8 3.1 collective-permute-start
  59.0 6.6 collective-permute-start.1
  69.7 4.6 collective-permute-done
  74.3 4.0 collective-permute-done.1
  78.3 3.4 pad_maximum_fusion
  81.7 4.8 gather_fusion.2
  90.6 34.4 %all-gather.6.cloned.1.call-done = bf16[24,192,256]{2,1,0:T(8,128)(2,1)} async-done(((bf16[3,192,256]{2,1,0:T(8,128)(2,1)}), bf16[24,192,256]{2,1,0:T(8,128)(2,1)}) %all-gather.6.cloned.1.call-update) | async-done | bytes 2359312 | tf_op jit(solution)/shard_map/all_gather | solution.py:18
  125.0 3.1 gather_fusion.3
  128.1 3.1 collective-permute-start.2
  131.2 3.1 gather_fusion.4
  134.3 6.6 collective-permute-start.3
  141.0 8.7 %collective-permute-done.2 = bf16[6,192,256]{2,1,0:T(8,128)(2,1)} collective-permute-done((bf16[6,192,256]{2,1,0:T(8,128)(2,1)}, bf16[6,192,256]{2,1,0:T(8,128)(2,1)}, u32[]{:S(2)}, u32[]{:S(2)}) %collective-permute-start.2) | collective-permute-done | bytes 589856 | tf_op jit(solution)/shard_map/ppermute | solution.py:10
  149.7 4.0 collective-permute-done.3
  153.7 3.3 pad_maximum_fusion.1
  157.0 4.8 gather_fusion.5
  166.1 34.3 %all-gather.8.cloned.1.call-done = bf16[24,192,256]{2,1,0:T(8,128)(2,1)} async-done(((bf16[3,192,256]{2,1,0:T(8,128)(2,1)}), bf16[24,192,256]{2,1,0:T(8,128)(2,1)}) %all-gather.8.cloned.1.call-update) | async-done | bytes 2359312 | tf_op jit(solution)/shard_map/all_gather | solution.py:18
  200.5 3.1 gather_fusion.6
  206.7 3.1 gather_fusion.7
  209.8 6.6 collective-permute-start.5
  216.4 3.2 fusion.42
  219.6 5.5 collective-permute-done.4
  225.1 4.0 collective-permute-done.5
  229.1 3.3 pad_maximum_fusion.2
  232.5 4.8 gather_fusion.8
  242.3 466.4 %all-reduce.4.cloned.1.call-done = (f32[256,256]{0,1:T(8,128)}, f32[256,256]{0,1:T(8,128)}) async-done(((f32[256,256]{0,1:T(8,128)}, f32[256,256]{0,1:T(8,128)}), (f32[256,256]{0,1:T(8,128)}, f32[256,256]{0,1:T(8,128)})) %all-reduce.4.cloned.1.call-update) | async-done | bytes 524304 | tf_op jit(solution)/shard_map/psum | solution.py:49
  714.8 13.2 %cholesky.50 = f32[128,128]{1,0:T(8,128)} custom-call(f32[128,128]{1,0:T(8,128)} %cholesky.118), custom_call_target="Cholesky" | custom-call | tf_op jit(solution)/shard_map/jit(cholesky)/cholesky | solution.py:52
  731.0 11.3 %custom-call.18 = f32[1,128,128]{1,2,0:T(8,128)} custom-call(f32[1,128,128]{2,1,0:T(8,128)} %get-tuple-element.48), custom_call_target="InvertDiagBlocksLowerTriangular" | custom-call | tf_op jit(solution)/shard_map/jit(cholesky)/cholesky | solution.py:52
  745.7 13.4 %cholesky.105 = f32[128,128]{1,0:T(8,128)} custom-call(f32[128,128]{1,0:T(8,128)} %convolution_subtract_fusion.3), custom_call_target="Cholesky" | custom-call | tf_op jit(solution)/shard_map/jit(cholesky)/cholesky | solution.py:52
  765.0 6.9 while.5
  771.8 21.1 %custom-call.19 = f32[2,128,128]{1,2,0:T(8,128)} custom-call(f32[2,128,128]{2,1,0:T(8,128)} %get-tuple-element.18), custom_call_target="InvertDiagBlocksLowerTriangular" | custom-call | tf_op jit(solution)/shard_map/jit(_solve_triangular)/triangular_solve | solution.py:53
  (77 shorter events, 62.4 us)
Async XLA Ops:
  7.2 79.4 %copy-start = (bf16[3,12,192,192]{3,2,1,0:T(8,128)(2,1)S(1)}, bf16[3,12,192,192]{3,2,1,0:T(8,128)(2,1)}, u32[]{:S(2)}) copy-start(bf16[3,12,192,192]{3,2,1,0:T(8,128)(2,1)} %param.9) | copy-start | bytes 7962628
  7.2 58.4 %copy-start.8 = (f32[2]{0:T(128)S(1)}, f32[2]{0:T(128)}, u32[]{:S(2)}) copy-start(f32[2]{0:T(128)} %param.13) | copy-start | bytes 28
  7.2 61.7 %copy-start.7 = (s32[3,12]{1,0:T(4,128)S(1)}, s32[3,12]{1,0:T(4,128)}, u32[]{:S(2)}) copy-start(s32[3,12]{1,0:T(4,128)} %param.10) | copy-start | bytes 436
  7.2 42.5 %all-gather.4.cloned.1.call-start = ((), (), s32[]{:S(2)}) async-start(), calls=%async_computation | async-start | bytes 2654208 | tf_op jit(solution)/shard_map/all_gather | solution.py:18
  9.2 115.8 %all-gather.6.cloned.1.call-start = ((), (), s32[]{:S(2)}) async-start(), calls=%async_computation.1 | async-start | bytes 2654208 | tf_op jit(solution)/shard_map/all_gather | solution.py:18
  52.8 21.5 %collective-permute-start = (bf16[6,192,256]{2,1,0:T(8,128)(2,1)}, bf16[6,192,256]{2,1,0:T(8,128)(2,1)}, u32[]{:S(2)}, u32[]{:S(2)}) collective-permute-start(bf16[6,192,256]{2,1,0:T(8,128)(2,1)} %gather_fusion), channel_id=1, source_target_pairs={{0,8},{8,16},{16,24},{24,32},{32,40},{40,48},{48,56},{56,64},{64,7... | collective-permute-start | bytes 1769480 | tf_op jit(solution)/shard_map/ppermute | solution.py:10
  59.0 19.3 %collective-permute-start.1 = (bf16[6,192,256]{2,1,0:T(8,128)(2,1)}, bf16[6,192,256]{2,1,0:T(8,128)(2,1)}, u32[]{:S(2)}, u32[]{:S(2)}) collective-permute-start(bf16[6,192,256]{2,1,0:T(8,128)(2,1)} %gather_fusion.1), channel_id=1, source_target_pairs={{0,504},{8,0},{16,8},{24,16},{32,24},{40,32},{48,40},{56,48},{64,5... | collective-permute-start | bytes 1769480 | tf_op jit(solution)/shard_map/ppermute | solution.py:10
  86.6 3.1 copy-start.2
  89.6 0.9 copy-start.4
  90.6 109.9 %all-gather.8.cloned.1.call-start = ((), (), s32[]{:S(2)}) async-start(), calls=%async_computation.2 | async-start | bytes 2654208 | tf_op jit(solution)/shard_map/all_gather | solution.py:18
  128.1 21.5 %collective-permute-start.2 = (bf16[6,192,256]{2,1,0:T(8,128)(2,1)}, bf16[6,192,256]{2,1,0:T(8,128)(2,1)}, u32[]{:S(2)}, u32[]{:S(2)}) collective-permute-start(bf16[6,192,256]{2,1,0:T(8,128)(2,1)} %gather_fusion.3), channel_id=1, source_target_pairs={{0,8},{8,16},{16,24},{24,32},{32,40},{40,48},{48,56},{56,64},{64,7... | collective-permute-start | bytes 1769480 | tf_op jit(solution)/shard_map/ppermute | solution.py:10
  134.3 19.3 %collective-permute-start.3 = (bf16[6,192,256]{2,1,0:T(8,128)(2,1)}, bf16[6,192,256]{2,1,0:T(8,128)(2,1)S(1)}, u32[]{:S(2)}, u32[]{:S(2)}) collective-permute-start(bf16[6,192,256]{2,1,0:T(8,128)(2,1)} %gather_fusion.4), channel_id=1, source_target_pairs={{0,504},{8,0},{16,8},{24,16},{32,24},{40,32},{48,40},{56,48},{64,5... | collective-permute-start | bytes 1769480 | tf_op jit(solution)/shard_map/ppermute | solution.py:10
  161.9 3.1 copy-start.3
  161.9 3.1 copy-start.5
  166.1 542.7 %all-reduce.4.cloned.1.call-start = ((), (), s32[]{:S(2)}) async-start(), calls=%async_computation.3 | async-start | bytes 1048576 | tf_op jit(solution)/shard_map/psum | solution.py:49
  203.6 21.5 %collective-permute-start.4 = (bf16[6,192,256]{2,1,0:T(8,128)(2,1)}, bf16[6,192,256]{2,1,0:T(8,128)(2,1)}, u32[]{:S(2)}, u32[]{:S(2)}) collective-permute-start(bf16[6,192,256]{2,1,0:T(8,128)(2,1)} %gather_fusion.6), channel_id=1, source_target_pairs={{0,8},{8,16},{16,24},{24,32},{32,40},{40,48},{48,56},{56,64},{64,7... | collective-permute-start | bytes 1769480 | tf_op jit(solution)/shard_map/ppermute | solution.py:10
  209.8 19.3 %collective-permute-start.5 = (bf16[6,192,256]{2,1,0:T(8,128)(2,1)}, bf16[6,192,256]{2,1,0:T(8,128)(2,1)S(1)}, u32[]{:S(2)}, u32[]{:S(2)}) collective-permute-start(bf16[6,192,256]{2,1,0:T(8,128)(2,1)} %gather_fusion.7), channel_id=1, source_target_pairs={{0,504},{8,0},{16,8},{24,16},{32,24},{40,32},{48,40},{56,48},{64,5... | collective-permute-start | bytes 1769480 | tf_op jit(solution)/shard_map/ppermute | solution.py:10
  237.3 3.0 copy-start.1
  713.5 0.7 copy-start.6
Sparse Core Ops, SparseCore 0:
  10.7 38.9 all-gather.3
  90.7 34.3 all-gather.5
  166.2 34.2 all-gather.7
  242.4 466.3 all-reduce.3
where the time goes:
time: 816 us; the launch traced here: 814 us
  waiting for transfers between devices  606 us (74%)
  other arithmetic  85.1 us (10%)
  local copies, waits for them, and re-layouts  47.2 us (6%)
  starting transfers between devices  29.3 us (4%)
  matrix products  29 us (4%)
  between operations  18 us (2%)
    psum x1, waiting for transfers between devices, local(): gram, cross = lax.psum((gram_part, cross_part), ('region', 'split'))  466 us
    all_gather x3, waiting for transfers between devices, apply_blocks(): region = lax.all_gather(shard_blocks, 'split', axis=0, tiled=True)  108 us
    another operation x7, other arithmetic, local(): lower = jnp.linalg.cholesky(gram)  42.1 us
    ppermute x6, waiting for transfers between devices, shifted(): return lax.ppermute(value, axis, pairs)  30.8 us
    ppermute x6, starting transfers between devices, shifted(): return lax.ppermute(value, axis, pairs)  29.1 us
    another operation x3, other arithmetic, local(): jax.scipy.linalg.solve_triangular(lower, filtered_two.T, lower=True)  22.8 us
  transfers between devices with their start and end apart: 10, of which 10 were waited for; matrix products, arithmetic and copies ran while one was open for 2% of the time, Pallas kernels for 0%

commit v1 on v0

--- a/solution.py
+++ b/solution.py
@@ -2,6 +2,11 @@
 import jax.numpy as jnp
 from jax import lax
 from jax.sharding import PartitionSpec as P
+
+
+def by_each_axis(array, axis_one, axis_two):
+    half = lax.psum(array, axis_one)
+    return lax.psum(half, axis_two)
 
 
 def shifted(value, axis, steps):
@@ -46,7 +51,7 @@
         filtered_two, filtered_two, contract, precision=lax.Precision.HIGHEST
     )
     cross_part = lax.dot_general(filtered_two, image, contract, precision=lax.Precision.HIGHEST)
-    gram, cross = lax.psum((gram_part, cross_part), ("region", "split"))
+    gram, cross = by_each_axis((gram_part, cross_part), "region", "split")
     gram = gram / total_rows
     cross = cross / total_rows
     lower = jnp.linalg.cholesky(gram)

time: 816 us -> 691 us (0.85)
  waiting for transfers between devices: 606 us -> 481 us
    psum x1 -> x2, waiting for transfers between devices: 466 us -> 341 us  [the longest x1 260 us: by_each_axis(): half = lax.psum(array, axis_one)]
  transfers between devices with their start and end apart: 10 -> 11, of which waited for: 10 -> 11; matrix products, arithmetic and copies ran while one was open for 2% -> 2% of each run, Pallas kernels for 0% -> 0%
where the time goes in v1:
time: 691 us; the launch traced here: 689 us
  waiting for transfers between devices  481 us (70%)
  other arithmetic  84.8 us (12%)
  local copies, waits for them, and re-layouts  47.1 us (7%)
  starting transfers between devices  29.5 us (4%)
  matrix products  29 us (4%)
  between operations  17.8 us (3%)
    psum x1, waiting for transfers between devices, by_each_axis(): half = lax.psum(array, axis_one)  260 us
    all_gather x3, waiting for transfers between devices, apply_blocks(): region = lax.all_gather(shard_blocks, 'split', axis=0, tiled=True)  108 us
    psum x1, waiting for transfers between devices, by_each_axis(): return lax.psum(half, axis_two)  81.7 us
    another operation x7, other arithmetic, local(): lower = jnp.linalg.cholesky(gram)  42 us
    ppermute x6, waiting for transfers between devices, shifted(): return lax.ppermute(value, axis, pairs)  31.1 us
    ppermute x6, starting transfers between devices, shifted(): return lax.ppermute(value, axis, pairs)  29.1 us
    another operation x3, other arithmetic, local(): jax.scipy.linalg.solve_triangular(lower, filtered_two.T, lower=True)  22.8 us
    gather x3, local copies, waits for them, and re-layouts, apply_blocks(): picked = candidates[block_cols]  14.5 us
  transfers between devices with their start and end apart: 11, of which 11 were waited for; matrix products, arithmetic and copies ran while one was open for 2% of the time, Pallas kernels for 0%

profile of v1, /device:TPU:1, one launch (start us, length us, event | category | flops | bytes accessed | tf_op | source)
XLA Modules:
  0.0 689.1 jit_solution(13045528527895492048)
XLA Ops:
  10.1 39.6 %all-gather.4.cloned.1.call-done = bf16[24,192,256]{2,1,0:T(8,128)(2,1)} async-done(((bf16[3,192,256]{2,1,0:T(8,128)(2,1)}), bf16[24,192,256]{2,1,0:T(8,128)(2,1)}) %all-gather.4.cloned.1.call-update) | async-done | bytes 2359312 | tf_op jit(solution)/shard_map/all_gather | solution.py:23
  49.7 3.1 gather_fusion
  52.8 3.1 collective-permute-start
  59.0 6.6 collective-permute-start.1
  69.5 4.9 collective-permute-done
  74.3 4.0 collective-permute-done.1
  78.3 3.4 pad_maximum_fusion
  81.7 4.8 gather_fusion.2
  90.6 34.4 %all-gather.6.cloned.1.call-done = bf16[24,192,256]{2,1,0:T(8,128)(2,1)} async-done(((bf16[3,192,256]{2,1,0:T(8,128)(2,1)}), bf16[24,192,256]{2,1,0:T(8,128)(2,1)}) %all-gather.6.cloned.1.call-update) | async-done | bytes 2359312 | tf_op jit(solution)/shard_map/all_gather | solution.py:23
  125.0 3.1 gather_fusion.3
  131.2 3.1 gather_fusion.4
  134.3 6.6 collective-permute-start.3
  140.9 8.7 %collective-permute-done.2 = bf16[6,192,256]{2,1,0:T(8,128)(2,1)} collective-permute-done((bf16[6,192,256]{2,1,0:T(8,128)(2,1)}, bf16[6,192,256]{2,1,0:T(8,128)(2,1)}, u32[]{:S(2)}, u32[]{:S(2)}) %collective-permute-start.2) | collective-permute-done | bytes 589856 | tf_op jit(solution)/shard_map/ppermute | solution.py:15
  149.6 4.0 collective-permute-done.3
  153.6 3.3 pad_maximum_fusion.1
  157.0 4.8 gather_fusion.5
  166.1 34.3 %all-gather.8.cloned.1.call-done = bf16[24,192,256]{2,1,0:T(8,128)(2,1)} async-done(((bf16[3,192,256]{2,1,0:T(8,128)(2,1)}), bf16[24,192,256]{2,1,0:T(8,128)(2,1)}) %all-gather.8.cloned.1.call-update) | async-done | bytes 2359312 | tf_op jit(solution)/shard_map/all_gather | solution.py:23
  200.4 3.1 gather_fusion.6
  206.6 3.1 gather_fusion.7
  209.7 6.6 collective-permute-start.5
  216.3 3.2 fusion.42
  219.5 5.5 collective-permute-done.4
  225.0 4.0 collective-permute-done.5
  229.0 3.3 pad_maximum_fusion.2
  232.3 4.8 gather_fusion.8
  242.4 259.7 %all-reduce.6.cloned.1.call-done = (f32[256,256]{0,1:T(8,128)}, f32[256,256]{0,1:T(8,128)}) async-done(((f32[256,256]{0,1:T(8,128)}, f32[256,256]{0,1:T(8,128)}), (f32[256,256]{0,1:T(8,128)}, f32[256,256]{0,1:T(8,128)})) %all-reduce.6.cloned.1.call-update) | async-done | bytes 524304 | tf_op jit(solution)/shard_map/psum | solution.py:8
  502.2 81.7 %all-reduce.8.cloned.1.call-done = (f32[256,256]{0,1:T(8,128)}, f32[256,256]{0,1:T(8,128)}) async-done(((f32[256,256]{0,1:T(8,128)}, f32[256,256]{0,1:T(8,128)}), (f32[256,256]{0,1:T(8,128)}, f32[256,256]{0,1:T(8,128)})) %all-reduce.8.cloned.1.call-update) | async-done | bytes 524304 | tf_op jit(solution)/shard_map/psum | solution.py:9
  589.9 13.2 %cholesky.50 = f32[128,128]{1,0:T(8,128)} custom-call(f32[128,128]{1,0:T(8,128)} %cholesky.118), custom_call_target="Cholesky" | custom-call | tf_op jit(solution)/shard_map/jit(cholesky)/cholesky | solution.py:57
  606.1 11.3 %custom-call.18 = f32[1,128,128]{1,2,0:T(8,128)} custom-call(f32[1,128,128]{2,1,0:T(8,128)} %get-tuple-element.50), custom_call_target="InvertDiagBlocksLowerTriangular" | custom-call | tf_op jit(solution)/shard_map/jit(cholesky)/cholesky | solution.py:57
  620.9 13.2 %cholesky.105 = f32[128,128]{1,0:T(8,128)} custom-call(f32[128,128]{1,0:T(8,128)} %convolution_subtract_fusion.3), custom_call_target="Cholesky" | custom-call | tf_op jit(solution)/shard_map/jit(cholesky)/cholesky | solution.py:57
  639.9 6.8 while.5
  646.7 21.1 %custom-call.19 = f32[2,128,128]{1,2,0:T(8,128)} custom-call(f32[2,128,128]{2,1,0:T(8,128)} %get-tuple-element.18), custom_call_target="InvertDiagBlocksLowerTriangular" | custom-call | tf_op jit(solution)/shard_map/jit(_solve_triangular)/triangular_solve | solution.py:58
  (80 shorter events, 65.6 us)
Async XLA Ops:
  7.2 79.4 %copy-start = (bf16[3,12,192,192]{3,2,1,0:T(8,128)(2,1)S(1)}, bf16[3,12,192,192]{3,2,1,0:T(8,128)(2,1)}, u32[]{:S(2)}) copy-start(bf16[3,12,192,192]{3,2,1,0:T(8,128)(2,1)} %param.9) | copy-start | bytes 7962628
  7.2 58.4 %copy-start.8 = (f32[2]{0:T(128)S(1)}, f32[2]{0:T(128)}, u32[]{:S(2)}) copy-start(f32[2]{0:T(128)} %param.13) | copy-start | bytes 28
  7.2 61.4 %copy-start.7 = (s32[3,12]{1,0:T(4,128)S(1)}, s32[3,12]{1,0:T(4,128)}, u32[]{:S(2)}) copy-start(s32[3,12]{1,0:T(4,128)} %param.10) | copy-start | bytes 436
  7.2 42.5 %all-gather.4.cloned.1.call-start = ((), (), s32[]{:S(2)}) async-start(), calls=%async_computation | async-start | bytes 2654208 | tf_op jit(solution)/shard_map/all_gather | solution.py:23
  9.2 115.8 %all-gather.6.cloned.1.call-start = ((), (), s32[]{:S(2)}) async-start(), calls=%async_computation.1 | async-start | bytes 2654208 | tf_op jit(solution)/shard_map/all_gather | solution.py:23
  52.8 21.5 %collective-permute-start = (bf16[6,192,256]{2,1,0:T(8,128)(2,1)}, bf16[6,192,256]{2,1,0:T(8,128)(2,1)}, u32[]{:S(2)}, u32[]{:S(2)}) collective-permute-start(bf16[6,192,256]{2,1,0:T(8,128)(2,1)} %gather_fusion), channel_id=1, source_target_pairs={{0,8},{8,16},{16,24},{24,32},{32,40},{40,48},{48,56},{56,64},{64,7... | collective-permute-start | bytes 1769480 | tf_op jit(solution)/shard_map/ppermute | solution.py:15
  59.0 19.3 %collective-permute-start.1 = (bf16[6,192,256]{2,1,0:T(8,128)(2,1)}, bf16[6,192,256]{2,1,0:T(8,128)(2,1)}, u32[]{:S(2)}, u32[]{:S(2)}) collective-permute-start(bf16[6,192,256]{2,1,0:T(8,128)(2,1)} %gather_fusion.1), channel_id=1, source_target_pairs={{0,504},{8,0},{16,8},{24,16},{32,24},{40,32},{48,40},{56,48},{64,5... | collective-permute-start | bytes 1769480 | tf_op jit(solution)/shard_map/ppermute | solution.py:15
  86.6 3.1 copy-start.2
  89.6 0.9 copy-start.4
  90.5 109.9 %all-gather.8.cloned.1.call-start = ((), (), s32[]{:S(2)}) async-start(), calls=%async_computation.2 | async-start | bytes 2654208 | tf_op jit(solution)/shard_map/all_gather | solution.py:23
  128.1 21.5 %collective-permute-start.2 = (bf16[6,192,256]{2,1,0:T(8,128)(2,1)}, bf16[6,192,256]{2,1,0:T(8,128)(2,1)}, u32[]{:S(2)}, u32[]{:S(2)}) collective-permute-start(bf16[6,192,256]{2,1,0:T(8,128)(2,1)} %gather_fusion.3), channel_id=1, source_target_pairs={{0,8},{8,16},{16,24},{24,32},{32,40},{40,48},{48,56},{56,64},{64,7... | collective-permute-start | bytes 1769480 | tf_op jit(solution)/shard_map/ppermute | solution.py:15
  134.3 19.3 %collective-permute-start.3 = (bf16[6,192,256]{2,1,0:T(8,128)(2,1)}, bf16[6,192,256]{2,1,0:T(8,128)(2,1)S(1)}, u32[]{:S(2)}, u32[]{:S(2)}) collective-permute-start(bf16[6,192,256]{2,1,0:T(8,128)(2,1)} %gather_fusion.4), channel_id=1, source_target_pairs={{0,504},{8,0},{16,8},{24,16},{32,24},{40,32},{48,40},{56,48},{64,5... | collective-permute-start | bytes 1769480 | tf_op jit(solution)/shard_map/ppermute | solution.py:15
  161.8 3.1 copy-start.3
  161.8 3.1 copy-start.5
  166.0 336.1 %all-reduce.6.cloned.1.call-start = ((), (), s32[]{:S(2)}) async-start(), calls=%async_computation.3 | async-start | bytes 1048576 | tf_op jit(solution)/shard_map/psum | solution.py:8
  203.5 21.5 %collective-permute-start.4 = (bf16[6,192,256]{2,1,0:T(8,128)(2,1)}, bf16[6,192,256]{2,1,0:T(8,128)(2,1)}, u32[]{:S(2)}, u32[]{:S(2)}) collective-permute-start(bf16[6,192,256]{2,1,0:T(8,128)(2,1)} %gather_fusion.6), channel_id=1, source_target_pairs={{0,8},{8,16},{16,24},{24,32},{32,40},{40,48},{48,56},{56,64},{64,7... | collective-permute-start | bytes 1769480 | tf_op jit(solution)/shard_map/ppermute | solution.py:15
  209.7 19.3 %collective-permute-start.5 = (bf16[6,192,256]{2,1,0:T(8,128)(2,1)}, bf16[6,192,256]{2,1,0:T(8,128)(2,1)S(1)}, u32[]{:S(2)}, u32[]{:S(2)}) collective-permute-start(bf16[6,192,256]{2,1,0:T(8,128)(2,1)} %gather_fusion.7), channel_id=1, source_target_pairs={{0,504},{8,0},{16,8},{24,16},{32,24},{40,32},{48,40},{56,48},{64,5... | collective-permute-start | bytes 1769480 | tf_op jit(solution)/shard_map/ppermute | solution.py:15
  237.2 3.0 copy-start.1
  242.2 341.7 %all-reduce.8.cloned.1.call-start = ((), (), s32[]{:S(2)}) async-start(), calls=%async_computation.4 | async-start | bytes 1048576 | tf_op jit(solution)/shard_map/psum | solution.py:9
  588.6 0.7 copy-start.6
Sparse Core Ops, SparseCore 0:
  10.7 38.9 all-gather.3
  90.6 34.3 all-gather.5
  166.1 34.2 all-gather.7
  242.3 259.7 all-reduce.5
  504.4 79.4 all-reduce.7
